TPU v7x, 256 devices: a whole 4x4x8 slice. The times are simulated.
256 devices in a mesh: row: 16 (over z, y_hi), col: 16 (over y_lo, x, core).
Axes of the slice: x: 4, y: 4 (y_hi: 2, y_lo: 2; y = y_hi * 2 + y_lo), z: 8, core: 2. Of those that a mesh axis runs over, the one named last changes fastest.
Arguments:
- anc_inverse: float32 [20480, 20480], P('row', 'col'), may hold values from -6 to 6
- l_store: float32 [16, 20480, 256], P('col', 'row'), may hold values from -0.0546875 to 0.0546875
- diag_inv: float32 [16, 256, 256], P('col'), may hold values from -6 to 6
- block_lists: int32 [4, 96], replicated, may hold values from 0 to 159, as said below
- block_counts: int32 [4], replicated, may hold values from 48 to 96, as said below
- sibling_columns: int32 [4], replicated, may hold values from 0 to 15, as said below
Outputs:
- upper_out: float32 [4, 256, 20480], P(None, 'row', 'col')
- lower_out: float32 [16, 20480, 256], P('col', 'row')
- diag_out: float32 [16, 256, 256], P('col')
Inputs may be any that keep to these rules, and one draw needn't show every extreme that they name: `block_lists`: in each sibling's row the entries are distinct block indices; entries at positions from block_counts onward are ignored. `block_counts`: some sibling uses all 96 entries. `sibling_columns`: distinct columns for distinct siblings.
All inputs are finite; a program needn't handle non-finite values.
Results may differ from a plain program's by a relative error of at most 0.00011.
Values sent between devices are 32-bit elements; how exact they have to be, the bound alone decides.
No kernel may reach another device: no remote copies, remote signals or barrier semaphores. Data moves between devices by JAX's collectives and lax.ppermute only.
A program may use at most 64 MiB of HBM per device.

v0:
```python
import jax
import jax.numpy as jnp
from jax import lax
from jax.sharding import Mesh
from jax.sharding import PartitionSpec as P

BLK = 128
ROW = ("row_0", "row_1")


def padded_to(lines, length):
    spare = -len(lines) % length
    return jnp.pad(lines, [(0, spare)] + [(0, 0)] * (lines.ndim - 1))


def total_of(x, axis):
    lines = x.reshape(-1, *x.shape[1:][-1:])
    padded = padded_to(lines, lax.axis_size(axis))
    own = lax.psum_scatter(padded, axis, scatter_dimension=0, tiled=True)
    whole = lax.all_gather(own, axis, axis=0, tiled=True)
    return whole[: len(lines)].reshape(x.shape)


def summed_rows(x, axes, dim):
    if not axes:
        return x
    nearer = lax.psum_scatter(x, axes[0], scatter_dimension=dim, tiled=True)
    return summed_rows(nearer, axes[1:], dim)


def joined_along(parts, dim):
    shape = list(parts.shape[1:])
    shape[dim] *= parts.shape[0]
    return jnp.moveaxis(parts, 0, dim).reshape(shape)


def from_everyone(x, axis):
    length = lax.axis_size(axis)
    return lax.all_to_all(jnp.broadcast_to(x[None], (length, *x.shape)), axis, 0, 0, tiled=True)


def collect(x, axis, dim):
    return joined_along(from_everyone(x, axis), dim)


def cut_along(x, dim, length):
    shape = x.shape
    parts = x.reshape(*shape[:dim], length, shape[dim] // length, *shape[dim + 1 :])
    return jnp.moveaxis(parts, dim, 0)


def sum_at_owner(x, axis, dim):
    length = lax.axis_size(axis)
    parts = lax.all_to_all(cut_along(x, dim, length), axis, 0, 0, tiled=True)
    return jnp.sum(parts, axis=0)


def nested_sum(x, axes):
    lines = x.reshape(-1, x.shape[-1])
    padded = padded_to(lines, lax.axis_size(axes))
    whole = collect(sum_at_owner(padded, axes, 0), axes, 0)
    return lax.slice_in_dim(whole, 0, len(lines)).reshape(x.shape)


def listed_blocks(block_lists, block_counts, first_block, block_total):
    block_ids = first_block + jnp.arange(block_total, dtype=jnp.int32)
    valid_entry = jnp.arange(block_lists.shape[1], dtype=jnp.int32)[None, :] < block_counts[:, None]
    entry_hits = (block_lists[:, :, None] == block_ids[None, None, :]) & valid_entry[:, :, None]
    return jnp.repeat(jnp.any(entry_hits, axis=1).astype(jnp.float32), BLK, axis=1)


def per_device(anc_inverse, l_store, diag_inv, block_lists, block_counts, sibling_columns):
    row_cells = anc_inverse.shape[0]
    col_cells = anc_inverse.shape[1]
    col_count = lax.axis_size("col")
    row_index = lax.axis_index(ROW)
    col_index = lax.axis_index("col")
    row_mask = listed_blocks(
        block_lists, block_counts, row_index * (row_cells // BLK), row_cells // BLK
    )
    col_mask = listed_blocks(
        block_lists, block_counts, col_index * (col_cells // BLK), col_cells // BLK
    )
    own_slot = l_store[0]
    chosen = (sibling_columns == col_index).astype(jnp.float32)
    placed = chosen[:, None, None] * own_slot[None]
    stacked = total_of(placed, "col")
    masked = stacked * row_mask[:, :, None]
    partial_value = (
        -jnp.einsum(
            "jrw,rc->jwc",
            masked,
            anc_inverse,
            precision=lax.Precision.HIGHEST,
            preferred_element_type=jnp.float32,
        )
        * col_mask[:, None, :]
    )
    upper_part = summed_rows(partial_value, ROW, 1)
    owner_table = (
        sibling_columns[:, None] == jnp.arange(col_count, dtype=jnp.int32)[None, :]
    ).astype(jnp.float32)
    slots = jnp.einsum(
        "jc,jwt->wct",
        owner_table,
        upper_part,
        precision=lax.Precision.HIGHEST,
        preferred_element_type=jnp.float32,
    )
    slots = slots.reshape(slots.shape[0], col_count * col_cells)
    by_owner = lax.all_to_all(slots, "col", split_axis=1, concat_axis=1, tiled=True)
    picked = lax.all_to_all(by_owner, ROW, split_axis=1, concat_axis=0, tiled=True)
    own_panel = jnp.sum(chosen[:, None, None] * masked, axis=0)
    inner_sum = jnp.dot(
        picked, own_panel, precision=lax.Precision.HIGHEST, preferred_element_type=jnp.float32
    )
    diag_total = nested_sum(inner_sum, ROW)
    present = jnp.sum(chosen)
    diag_out = (present * diag_inv[0] - diag_total)[None]
    lower_out = jnp.transpose(picked)[None]
    return (upper_part, lower_out, diag_out)


def solution(mesh):
    finer = Mesh(mesh.devices.reshape(8, 2, mesh.shape["col"]), ("row_0", "row_1", "col"))
    return jax.shard_map(
        per_device,
        mesh=finer,
        in_specs=(P(ROW, "col"), P("col", ROW, None), P("col", None, None), P(), P(), P()),
        out_specs=(P(None, ROW, "col"), P("col", ROW, None), P("col", None, None)),
        check_vma=False,
    )
```

profile of v0, /device:TPU:2, one launch (start us, length us, event | category | flops | bytes accessed | tf_op | source)
XLA Modules:
  0.0 359.1 jit_solution(242088408683245852)
XLA Ops:
  7.2 0.0 reduce-scatter.4.cloned.1.call-start
  7.2 1.3 fusion.15
  8.5 0.1 mul.66
  8.6 4.4 %bitcast_multiply_fusion = f32[5120,256]{1,0:T(8,128)} fusion(f32[1280,256]{1,0:T(8,128)} %bitcast.42, f32[5120]{0:T(1024)S(1)} %mul.67), kind=kLoop, calls=%fused_computation.2 | loop fusion | flops 1310720 | bytes 6574080 | tf_op jit(solution)/shard_map/mul | solution.py:86
  13.0 0.0 reduce-scatter.4.cloned.1.call-update
  13.0 0.0 all-gather.2.cloned.1.call-start
  13.1 70.1 %reduce-scatter.4.cloned.1.call-done = f32[320,256]{1,0:T(8,128)} async-done(((f32[5120,256]{1,0:T(8,128)}), f32[320,256]{1,0:T(8,128)}) %reduce-scatter.4.cloned.1.call-update) | async-done | bytes 327696 | tf_op jit(solution)/shard_map/reduce_scatter | solution.py:19
  83.2 0.0 reduce-scatter.6.cloned.1.call-start
  83.3 0.1 iota_compare_fusion.1
  83.4 0.5 and_reduce_fusion.1
  83.9 0.1 copy.32
  84.0 0.1 broadcast_bitcast_fusion.1
  84.1 0.1 copy.34
  84.2 0.1 broadcast_bitcast_fusion
  84.3 44.9 %all-gather.2.cloned.1.call-done = f32[5120,256]{1,0:T(8,128)} async-done(((f32[320,256]{1,0:T(8,128)}), f32[5120,256]{1,0:T(8,128)}) %all-gather.2.cloned.1.call-update) | async-done | bytes 5242896 | tf_op jit(solution)/shard_map/all_gather | solution.py:20
  129.2 28.0 %negate_multiply_fusion = f32[4,256,1280]{2,1,0:T(8,128)} fusion(f32[1280,1280]{1,0:T(8,128)} %param.6, f32[4,1280,256]{2,1,0:T(8,128)} %bitcast.40, f32[4,1280]{1,0:T(4,128)S(1)} %bitcast.46, f32[4,1280]{1,0:T(4,128)S(1)} %bitcast.44), kind=kOutput, calls=%fused_computation.4 | convolution fusion | flops 20136591360 | bytes 17080320 | tf_op jit(solution)/shard_map/jrw,rc->jwc/dot_general | solution.py:90
  157.2 0.2 reduce-scatter.8.cloned.1.call-start
  157.4 66.1 %reduce-scatter.6.cloned.1.call-done = f32[4,32,1280]{2,1,0:T(8,128)} async-done(((f32[4,256,1280]{2,1,0:T(8,128)}), f32[4,32,1280]{2,1,0:T(8,128)}) %reduce-scatter.6.cloned.1.call-update) | async-done | bytes 655376 | tf_op jit(solution)/shard_map/reduce_scatter | solution.py:27
  223.5 24.2 %reduce-scatter.8.cloned.1.call-done = f32[4,16,1280]{2,1,0:T(8,128)} async-done(((f32[4,32,1280]{2,1,0:T(8,128)}), f32[4,16,1280]{2,1,0:T(8,128)}) %reduce-scatter.8.cloned.1.call-update) | async-done | bytes 327696 | tf_op jit(solution)/shard_map/reduce_scatter | solution.py:27
  247.7 1.8 convolution_bitcast_fusion
  249.5 0.8 copy.36
  250.3 21.4 %all_to_all.32 = f32[16,16,1280]{2,0,1:T(8,128)} all-to-all(f32[16,16,1280]{2,0,1:T(8,128)S(1)} %copy.36), channel_id=1, replica_groups=mesh['row_0'=8,'row_1'=2,'col'=16] {'col'}, dimensions={1} | all-to-all | bytes 2621440 | tf_op jit(solution)/shard_map/all_to_all | solution.py:111
  271.7 8.6 %all-to-all-start.1 = ((f32[16,16,1280]{2,0,1:T(8,128)}), f32[16,16,1280]{2,0,1:T(8,128)S(1)}, u32[]{:S(2)}, u32[]{:S(2)}) async-start(f32[16,16,1280]{2,0,1:T(8,128)} %all_to_all.32), calls=%async_computation.4 | async-start | bytes 2621440 | tf_op jit(solution)/shard_map/all_to_all | solution.py:112
  280.3 3.1 multiply_reduce_fusion
  283.4 33.1 %all-to-all-done.1 = f32[16,16,1280]{2,0,1:T(8,128)S(1)} async-done(((f32[16,16,1280]{2,0,1:T(8,128)}), f32[16,16,1280]{2,0,1:T(8,128)S(1)}, u32[]{:S(2)}, u32[]{:S(2)}) %all-to-all-start.1) | async-done | bytes 1310752 | tf_op jit(solution)/shard_map/all_to_all | solution.py:112
  316.5 1.2 fusion.8
  317.8 17.0 %all_to_all.33 = f32[16,16,256]{2,1,0:T(8,128)S(1)} all-to-all(f32[16,16,256]{2,1,0:T(8,128)S(1)} %fusion.8), channel_id=1, replica_groups=mesh['row_0'=8,'row_1'=2,'col'=16] {'row_0','row_1'}, dimensions={0} | all-to-all | bytes 524288 | tf_op jit(solution)/shard_map/all_to_all | solution.py:54
  334.8 0.7 broadcast_in_dim.11
  335.5 3.5 all-to-all-start.3
  339.1 1.5 copy.37
  340.5 10.7 %all-to-all-done.3 = f32[16,16,256]{2,1,0:T(8,128)S(1)} async-done(((f32[16,16,256]{2,1,0:T(8,128)}), f32[16,16,256]{2,1,0:T(8,128)S(1)}, u32[]{:S(2)}, u32[]{:S(2)}) %all-to-all-start.3) | async-done | bytes 262176 | tf_op jit(solution)/shard_map/all_to_all | solution.py:39
  351.2 1.3 bitcast_subtract_fusion
  (18 shorter events, 0.2 us)
Async XLA Ops:
  7.2 76.0 %reduce-scatter.4.cloned.1.call-start = ((), (), s32[]{:S(2)}) async-start(), calls=%async_computation.7 | async-start | bytes 5570560 | tf_op jit(solution)/shard_map/reduce_scatter | solution.py:19
  8.6 74.7 %copy-start.3 = (s32[4]{0:T(128)S(1)}, s32[4]{0:T(128)}, u32[]{:S(2)}) copy-start(s32[4]{0:T(128)} %param.10) | copy-start | bytes 52
  8.6 74.8 %copy-start.2 = (s32[4,96]{1,0:T(4,128)S(1)}, s32[4,96]{1,0:T(4,128)}, u32[]{:S(2)}) copy-start(s32[4,96]{1,0:T(4,128)} %param.9) | copy-start | bytes 4612
  13.0 116.1 %all-gather.2.cloned.1.call-start = ((), (), s32[]{:S(2)}) async-start(), calls=%async_computation.8 | async-start | bytes 5570560 | tf_op jit(solution)/shard_map/all_gather | solution.py:20
  83.2 140.3 %reduce-scatter.6.cloned.1.call-start = ((), (), s32[]{:S(2)}) async-start(), calls=%async_computation.9 | async-start | bytes 5898240 | tf_op jit(solution)/shard_map/reduce_scatter | solution.py:27
  157.2 90.5 %copy-start.1 = (s32[4]{0:T(128)S(1)}, s32[4]{0:T(128)}, u32[]{:S(2)}) copy-start(s32[4]{0:T(128)} %param.11) | copy-start | bytes 52
  157.2 90.5 %reduce-scatter.8.cloned.1.call-start = ((), (), s32[]{:S(2)}) async-start(), calls=%async_computation.10 | async-start | bytes 983040 | tf_op jit(solution)/shard_map/reduce_scatter | solution.py:27
  271.7 44.8 %all-to-all-start.1 = ((f32[16,16,1280]{2,0,1:T(8,128)}), f32[16,16,1280]{2,0,1:T(8,128)S(1)}, u32[]{:S(2)}, u32[]{:S(2)}) async-start(f32[16,16,1280]{2,0,1:T(8,128)} %all_to_all.32), calls=%async_computation.4 | async-start | bytes 2621440 | tf_op jit(solution)/shard_map/all_to_all | solution.py:112
  280.3 70.9 %copy-start = (f32[1,256,256]{2,1,0:T(8,128)S(1)}, f32[1,256,256]{2,1,0:T(8,128)}, u32[]{:S(2)}) copy-start(f32[1,256,256]{2,1,0:T(8,128)} %param.8) | copy-start | bytes 786436
  335.5 15.7 %all-to-all-start.3 = ((f32[16,16,256]{2,1,0:T(8,128)}), f32[16,16,256]{2,1,0:T(8,128)S(1)}, u32[]{:S(2)}, u32[]{:S(2)}) async-start(f32[16,16,256]{2,1,0:T(8,128)} %broadcast_in_dim.11), calls=%async_computation.6 | async-start | bytes 524288 | tf_op jit(solution)/shard_map/all_to_all | solution.py:39
Sparse Core Ops, SparseCore 0:
  13.1 70.0 reduce-scatter.3
  85.0 44.0 all-gather.1
  157.3 66.1 reduce-scatter.5
  226.4 21.2 reduce-scatter.7
where the time goes:
time: 360 us; the launch traced here: 359 us
  waiting for transfers between devices  249 us (69%)
  blocking collectives  38.4 us (11%)
  matrix products  31.1 us (9%)
  between operations  13.9 us (4%)
  starting transfers between devices  12.5 us (3%)
  other arithmetic  10.7 us (3%)
    reduce_scatter x2, waiting for transfers between devices, summed_rows(): nearer = lax.psum_scatter(x, axes[0], scatter_dimension=dim, tiled=True)  90.2 us
    reduce_scatter x1, waiting for transfers between devices, total_of(): own = lax.psum_scatter(padded, axis, scatter_dimension=0, tiled=True)  70.1 us
    all_gather x1, waiting for transfers between devices, total_of(): whole = lax.all_gather(own, axis, axis=0, tiled=True)  44.9 us
    all_to_all x1, waiting for transfers between devices, per_device(): lax.all_to_all(by_owner, ROW, split_axis=1, concat_axis=0, tiled=True)  33.1 us
    dot_general x1, matrix products, per_device(): jnp.einsum('jrw,rc->jwc', masked, anc_inverse, precision=lax.Precision.HI...  28 us
    all_to_all x1, blocking collectives, per_device(): lax.all_to_all(slots, 'col', split_axis=1, concat_axis=1, tiled=True)  21.4 us
    all_to_all x1, blocking collectives, sum_at_owner(): parts = lax.all_to_all(cut_along(x, dim, length), axis, 0, 0, tiled=True)  17 us
    all_to_all x1, waiting for transfers between devices, from_everyone(): lax.all_to_all(jnp.broadcast_to(x[None], (length, *x.shape)), axis, 0, 0,...  10.7 us
  transfers between devices with their start and end apart: 6, of which 6 were waited for; matrix products, arithmetic and copies ran while one was open for 2% of the time, Pallas kernels for 0%

commit v1 on v0

--- a/solution.py
+++ b/solution.py
@@ -17,7 +17,9 @@
     lines = x.reshape(-1, *x.shape[1:][-1:])
     padded = padded_to(lines, lax.axis_size(axis))
     own = lax.psum_scatter(padded, axis, scatter_dimension=0, tiled=True)
-    whole = lax.all_gather(own, axis, axis=0, tiled=True)
+    whole = jnp.concatenate(
+        lax.all_to_all(jnp.stack([own] * lax.axis_size(axis)), axis, 0, 0), axis=0
+    )
     return whole[: len(lines)].reshape(x.shape)
 
 

time: 360 us -> 417 us (1.16)
  blocking collectives: 38.4 us -> 83 us
  matrix products: 31.1 us -> 48.4 us
  waiting for transfers between devices: 249 us -> 240 us
    all_to_all x0 -> x1, blocking collectives: none -> 45.7 us  [per_device(): lax.all_to_all(by_owner, ROW, split_axis=1, concat_axis=0, tiled=True)]
    all_gather x1 -> x0, waiting for transfers between devices: 44.9 us -> none  [total_of(): whole = lax.all_gather(own, axis, axis=0, tiled=True)]
    all_to_all x1, waiting for transfers between devices: 33.1 us -> 69.9 us  [total_of(): lax.all_to_all(jnp.stack([own] * lax.axis_size(axis)), axis, 0, 0)]
    dot_general x1, matrix products: 28 us -> 45.4 us  [per_device(): jnp.einsum('jrw,rc->jwc', masked, anc_inverse, precision=lax.Precision.HI...]
  transfers between devices with their start and end apart: 6 -> 5, of which waited for: 6 -> 5; matrix products, arithmetic and copies ran while one was open for 2% -> 1% of each run, Pallas kernels for 0% -> 0%
where the time goes in v1:
time: 417 us; the launch traced here: 416 us
  waiting for transfers between devices  240 us (58%)
  blocking collectives  83 us (20%)
  matrix products  48.4 us (12%)
  between operations  13.8 us (3%)
  starting transfers between devices  13.1 us (3%)
  other arithmetic  10.8 us (3%)
  local copies, waits for them, and re-layouts  7.24 us (2%)
    reduce_scatter x2, waiting for transfers between devices, summed_rows(): nearer = lax.psum_scatter(x, axes[0], scatter_dimension=dim, tiled=True)  88.9 us
    reduce_scatter x1, waiting for transfers between devices, total_of(): own = lax.psum_scatter(padded, axis, scatter_dimension=0, tiled=True)  70.2 us
    all_to_all x1, waiting for transfers between devices, total_of(): lax.all_to_all(jnp.stack([own] * lax.axis_size(axis)), axis, 0, 0)  69.9 us
    all_to_all x1, blocking collectives, per_device(): lax.all_to_all(by_owner, ROW, split_axis=1, concat_axis=0, tiled=True)  45.7 us
    dot_general x1, matrix products, per_device(): jnp.einsum('jrw,rc->jwc', masked, anc_inverse, precision=lax.Precision.HI...  45.4 us
    all_to_all x1, blocking collectives, per_device(): lax.all_to_all(slots, 'col', split_axis=1, concat_axis=1, tiled=True)  21.3 us
    all_to_all x1, blocking collectives, sum_at_owner(): parts = lax.all_to_all(cut_along(x, dim, length), axis, 0, 0, tiled=True)  16 us
    all_to_all x1, waiting for transfers between devices, from_everyone(): lax.all_to_all(jnp.broadcast_to(x[None], (length, *x.shape)), axis, 0, 0,...  10.7 us
  transfers between devices with their start and end apart: 5, of which 5 were waited for; matrix products, arithmetic and copies ran while one was open for 1% of the time, Pallas kernels for 0%

profile of v1, /device:TPU:2, one launch (start us, length us, event | category | flops | bytes accessed | tf_op | source)
XLA Modules:
  0.0 416.2 jit_solution(5093060180059555187)
XLA Ops:
  7.2 0.0 reduce-scatter.4.cloned.1.call-start
  7.2 1.3 fusion.11
  8.5 0.1 mul.66
  8.6 4.4 %bitcast_multiply_fusion.1 = f32[5120,256]{1,0:T(8,128)} fusion(f32[1280,256]{1,0:T(8,128)} %bitcast.43, f32[5120]{0:T(1024)S(1)} %mul.67), kind=kLoop, calls=%fused_computation.3 | loop fusion | flops 1310720 | bytes 6574080 | tf_op jit(solution)/shard_map/mul | solution.py:88
  13.0 0.0 reduce-scatter.4.cloned.1.call-update
  13.0 70.2 %reduce-scatter.4.cloned.1.call-done = f32[320,256]{1,0:T(8,128)} async-done(((f32[5120,256]{1,0:T(8,128)}), f32[320,256]{1,0:T(8,128)}) %reduce-scatter.4.cloned.1.call-update) | async-done | bytes 327696 | tf_op jit(solution)/shard_map/reduce_scatter | solution.py:19
  83.2 3.8 stack.2
  87.0 9.2 %all-to-all-start = ((f32[16,320,256]{2,1,0:T(8,128)}), f32[16,320,256]{2,1,0:T(8,128)}, u32[]{:S(2)}, u32[]{:S(2)}) async-start(f32[16,320,256]{2,1,0:T(8,128)} %stack.2), calls=%async_computation.1 | async-start | bytes 10485760 | tf_op jit(solution)/shard_map/all_to_all | solution.py:21
  96.2 0.0 reduce-scatter.6.cloned.1.call-start
  96.3 0.1 iota_compare_fusion.1
  96.4 0.5 and_reduce_fusion
  96.9 0.1 copy.32
  97.0 0.1 broadcast_bitcast_fusion.1
  97.1 0.1 copy.34
  97.2 0.1 broadcast_bitcast_fusion
  97.3 69.9 %all-to-all-done = f32[16,320,256]{2,1,0:T(8,128)} async-done(((f32[16,320,256]{2,1,0:T(8,128)}), f32[16,320,256]{2,1,0:T(8,128)}, u32[]{:S(2)}, u32[]{:S(2)}) %all-to-all-start) | async-done | bytes 5242912 | tf_op jit(solution)/shard_map/all_to_all | solution.py:21
  167.2 3.1 multiply_reduce_fusion
  170.3 45.4 %negate_multiply_fusion = f32[4,256,1280]{2,1,0:T(8,128)} fusion(f32[4,1280,256]{2,1,0:T(8,128)S(1)} %get-tuple-element.23, f32[1280,1280]{1,0:T(8,128)} %param.6, f32[4,1280]{1,0:T(4,128)S(1)} %bitcast.46), kind=kOutput, calls=%fused_computation.5 | convolution fusion | flops 20135280640 | bytes 17059840 | tf_op jit(solution)/shard_map/jrw,rc->jwc/dot_general | solution.py:92
  215.7 0.2 reduce-scatter.8.cloned.1.call-start
  216.0 64.6 %reduce-scatter.6.cloned.1.call-done = f32[4,32,1280]{2,1,0:T(8,128)} async-done(((f32[4,256,1280]{2,1,0:T(8,128)}), f32[4,32,1280]{2,1,0:T(8,128)}) %reduce-scatter.6.cloned.1.call-update) | async-done | bytes 655376 | tf_op jit(solution)/shard_map/reduce_scatter | solution.py:29
  280.6 24.3 %reduce-scatter.8.cloned.1.call-done = f32[4,16,1280]{2,1,0:T(8,128)} async-done(((f32[4,32,1280]{2,1,0:T(8,128)}), f32[4,16,1280]{2,1,0:T(8,128)}) %reduce-scatter.8.cloned.1.call-update) | async-done | bytes 327696 | tf_op jit(solution)/shard_map/reduce_scatter | solution.py:29
  304.9 1.8 convolution_bitcast_fusion
  306.8 0.8 copy.36
  307.5 21.3 %all_to_all.37 = f32[16,16,1280]{2,0,1:T(8,128)S(1)} all-to-all(f32[16,16,1280]{2,0,1:T(8,128)S(1)} %copy.36), channel_id=1, replica_groups=mesh['row_0'=8,'row_1'=2,'col'=16] {'col'}, dimensions={1} | all-to-all | bytes 2621440 | tf_op jit(solution)/shard_map/all_to_all | solution.py:113
  328.8 45.7 %all_to_all.38 = f32[16,16,1280]{2,0,1:T(8,128)S(1)} all-to-all(f32[16,16,1280]{2,0,1:T(8,128)S(1)} %all_to_all.37), channel_id=1, replica_groups=mesh['row_0'=8,'row_1'=2,'col'=16] {'row_0','row_1'}, dimensions={1} | all-to-all | bytes 2621440 | tf_op jit(solution)/shard_map/all_to_all | solution.py:114
  374.6 1.2 fusion.4
  375.8 16.0 %all_to_all.39 = f32[16,16,256]{2,1,0:T(8,128)S(1)} all-to-all(f32[16,16,256]{2,1,0:T(8,128)S(1)} %fusion.4), channel_id=1, replica_groups=mesh['row_0'=8,'row_1'=2,'col'=16] {'row_0','row_1'}, dimensions={0} | all-to-all | bytes 524288 | tf_op jit(solution)/shard_map/all_to_all | solution.py:56
  391.8 0.7 broadcast_in_dim.11
  392.6 3.5 all-to-all-start.4
  396.1 1.5 copy.37
  397.6 10.7 %all-to-all-done.4 = f32[16,16,256]{2,1,0:T(8,128)S(1)} async-done(((f32[16,16,256]{2,1,0:T(8,128)}), f32[16,16,256]{2,1,0:T(8,128)S(1)}, u32[]{:S(2)}, u32[]{:S(2)}) %all-to-all-start.4) | async-done | bytes 262176 | tf_op jit(solution)/shard_map/all_to_all | solution.py:41
  408.3 1.4 bitcast_subtract_fusion
  (17 shorter events, 0.1 us)
Async XLA Ops:
  7.2 76.0 %reduce-scatter.4.cloned.1.call-start = ((), (), s32[]{:S(2)}) async-start(), calls=%async_computation.8 | async-start | bytes 5570560 | tf_op jit(solution)/shard_map/reduce_scatter | solution.py:19
  87.0 9.3 %copy-start.3 = (s32[4]{0:T(128)S(1)}, s32[4]{0:T(128)}, u32[]{:S(2)}) copy-start(s32[4]{0:T(128)} %param.10) | copy-start | bytes 52
  87.0 9.4 %copy-start.2 = (s32[4,96]{1,0:T(4,128)S(1)}, s32[4,96]{1,0:T(4,128)}, u32[]{:S(2)}) copy-start(s32[4,96]{1,0:T(4,128)} %param.9) | copy-start | bytes 4612
  87.0 80.3 %all-to-all-start = ((f32[16,320,256]{2,1,0:T(8,128)}), f32[16,320,256]{2,1,0:T(8,128)}, u32[]{:S(2)}, u32[]{:S(2)}) async-start(f32[16,320,256]{2,1,0:T(8,128)} %stack.2), calls=%async_computation.1 | async-start | bytes 10485760 | tf_op jit(solution)/shard_map/all_to_all | solution.py:21
  96.2 184.3 %reduce-scatter.6.cloned.1.call-start = ((), (), s32[]{:S(2)}) async-start(), calls=%async_computation.9 | async-start | bytes 5898240 | tf_op jit(solution)/shard_map/reduce_scatter | solution.py:29
  215.7 89.2 %copy-start.1 = (s32[4]{0:T(128)S(1)}, s32[4]{0:T(128)}, u32[]{:S(2)}) copy-start(s32[4]{0:T(128)} %param.11) | copy-start | bytes 52
  215.7 89.2 %reduce-scatter.8.cloned.1.call-start = ((), (), s32[]{:S(2)}) async-start(), calls=%async_computation.10 | async-start | bytes 983040 | tf_op jit(solution)/shard_map/reduce_scatter | solution.py:29
  328.8 79.5 %copy-start = (f32[1,256,256]{2,1,0:T(8,128)S(1)}, f32[1,256,256]{2,1,0:T(8,128)}, u32[]{:S(2)}) copy-start(f32[1,256,256]{2,1,0:T(8,128)} %param.8) | copy-start | bytes 786436
  392.6 15.7 %all-to-all-start.4 = ((f32[16,16,256]{2,1,0:T(8,128)}), f32[16,16,256]{2,1,0:T(8,128)S(1)}, u32[]{:S(2)}, u32[]{:S(2)}) async-start(f32[16,16,256]{2,1,0:T(8,128)} %broadcast_in_dim.11), calls=%async_computation.7 | async-start | bytes 524288 | tf_op jit(solution)/shard_map/all_to_all | solution.py:41
Sparse Core Ops, SparseCore 0:
  13.1 70.0 reduce-scatter.3
  215.9 64.6 reduce-scatter.5
  283.6 21.2 reduce-scatter.7
